TPU v7x, 128 devices: a whole 4x4x4 slice. The times are simulated.
128 devices in a mesh: aux: 4 (over y_lo, core), pair: 32 (over z, y_hi, x).
Axes of the slice: x: 4, y: 4 (y_hi: 2, y_lo: 2; y = y_hi * 2 + y_lo), z: 4, core: 2. Of those that a mesh axis runs over, the one named last changes fastest.
Arguments:
- amplitudes: bfloat16 [65536, 512], P('pair', 'aux'), may hold values from -4 to 4
- coulomb: bfloat16 [65536, 512], P('pair'), may hold values from -12 to 12
- df_factors: bfloat16 [65536, 2048], P('pair', 'aux'), may hold values from -0.07861328 to 0.07861328
- thc_left: bfloat16 [512, 1536], P('pair', 'aux'), may hold values from -0.50390625 to 0.50390625
- thc_right: bfloat16 [512, 1536], P('pair', 'aux'), may hold values from -0.50390625 to 0.50390625
- occ_energy: float32 [128], P('pair'), may hold values from -2 to -0.5
- vir_energy: float32 [512], replicated, may hold values from 0.5 to 3
- pivot_energy: float32 [1], replicated, may hold values from -2 to -0.5
Outputs:
- updated: bfloat16 [65536, 512], P('pair', 'aux')
All inputs are finite; a program needn't handle non-finite values.
Results may differ from a plain program's by a relative error of at most 0.0051.
Values may be sent and summed in bfloat16 or wider, within the bound.
A program may use at most 64 MiB of HBM per device.

v0:
```python
import jax
import jax.numpy as jnp
from jax import lax
from jax.sharding import PartitionSpec as P

ITERS = 2


def per_device(
    amplitudes, coulomb, df_factors, thc_left, thc_right, occ_energy, vir_energy, pivot_energy
):
    column_index = lax.axis_index("aux")
    width = amplitudes.shape[1]
    rows = amplitudes.shape[0]
    nvirt = vir_energy.shape[0]
    nocc_local = rows // nvirt
    denom_full = (
        vir_energy[None, :, None]
        + vir_energy[None, None, :]
        - occ_energy[:, None, None]
        - pivot_energy[0]
    ).reshape(rows, nvirt)
    local = amplitudes
    whole = None
    for step in range(ITERS):
        whole = lax.all_gather(local, "aux", axis=1, tiled=True)
        left, right = (
            lax.all_gather(thc_left, "pair", axis=0, tiled=True),
            lax.all_gather(thc_right, "pair", axis=0, tiled=True),
        )
        gram = lax.dot_general(
            df_factors, whole, (((0,), (0,)), ((), ())), preferred_element_type=jnp.float32
        )
        gram = lax.psum(gram, "pair").astype(jnp.bfloat16)
        proj = jnp.dot(whole, right, preferred_element_type=jnp.float32).reshape(
            nocc_local, nvirt, right.shape[1]
        )
        middle = jnp.sum(proj * left.astype(jnp.float32)[None], axis=1)
        weighted = (
            (left.astype(jnp.float32)[None] * middle[:, None, :])
            .astype(jnp.bfloat16)
            .reshape(rows, right.shape[1])
        )
        ladder = lax.dot_general(
            weighted, right, (((1,), (1,)), ((), ())), preferred_element_type=jnp.float32
        )
        cycle = jnp.dot(df_factors, gram, preferred_element_type=jnp.float32)
        part = cycle + ladder
        share = lax.psum_scatter(part, "aux", scatter_dimension=1, tiled=True)
        coulomb_block = lax.dynamic_slice_in_dim(coulomb, column_index * width, width, 1)
        denom_block = lax.dynamic_slice_in_dim(denom_full, column_index * width, width, 1)
        local = ((coulomb_block.astype(jnp.float32) + share) / denom_block).astype(jnp.bfloat16)
        whole = None
    return local


def solution(mesh):
    in_specs = (
        P("pair", "aux"),
        P("pair", None),
        P("pair", "aux"),
        P("pair", "aux"),
        P("pair", "aux"),
        P("pair"),
        P(),
        P(),
    )
    out_specs = P("pair", "aux")
    return jax.shard_map(
        per_device, mesh=mesh, in_specs=in_specs, out_specs=out_specs, check_vma=False
    )
```

profile of v0, /device:TPU:1, one launch (start us, length us, event | category | flops | bytes accessed | tf_op | source)
XLA Modules:
  0.0 727.8 jit_solution(6331696356727031182)
XLA Ops:
  7.3 85.5 %all_gather.15 = bf16[512,384]{1,0:T(8,128)(2,1)S(1)} all-gather(bf16[16,384]{1,0:T(8,128)(2,1)} %param.11), channel_id=1, replica_groups=mesh['aux'=4,'pair'=32] {'pair'}, dimensions={0}, use_global_device_ids=true | all-gather | bytes 405504 | tf_op jit(solution)/shard_map/all_gather | solution.py:28
  92.9 75.5 %all_gather.16 = bf16[512,384]{1,0:T(8,128)(2,1)S(1)} all-gather(bf16[16,384]{1,0:T(8,128)(2,1)S(1)} %copy-done.6), channel_id=1, replica_groups=mesh['aux'=4,'pair'=32] {'pair'}, dimensions={0}, use_global_device_ids=true | all-gather | bytes 405504 | tf_op jit(solution)/shard_map/all_gather | solution.py:29
  168.3 3.0 multiply_reduce_fusion.1
  171.3 1.5 multiply_convert_fusion.1
  172.8 2.3 fusion.9
  175.1 162.7 %all-reduce.2 = bf16[512,512]{1,0:T(8,128)(2,1)} all-reduce(f32[512,512]{1,0:T(8,128)} %fusion.9), channel_id=1, replica_groups=mesh['aux'=4,'pair'=32] {'pair'}, use_global_device_ids=true, to_apply=%region_0.0 | all-reduce | flops 262144 | bytes 1572864 | tf_op jit(solution)/shard_map/psum | solution.py:34
  337.7 2.5 fusion.11
  340.2 3.3 bitcast_add_fusion.1
  343.6 1.9 constant_dynamic-slice_fusion
  345.5 2.0 copy.15
  347.7 0.7 sub.27
  348.4 3.9 copy.17
  353.0 86.1 %reduce-scatter.3.cloned.1.call-done = f32[2048,128]{0,1:T(8,128)} async-done(((f32[2048,512]{0,1:T(8,128)}), f32[2048,128]{0,1:T(8,128)}) %reduce-scatter.3.cloned.1.call-update) | async-done | bytes 1048592 | tf_op jit(solution)/shard_map/reduce_scatter | solution.py:49
  439.1 2.7 fusion.1
  441.9 30.3 %all-gather.5.cloned.1.call-done = bf16[2048,512]{0,1:T(8,128)(2,1)} async-done(((bf16[2048,128]{0,1:T(8,128)(2,1)}), bf16[2048,512]{0,1:T(8,128)(2,1)}) %all-gather.5.cloned.1.call-update) | async-done | bytes 2097168 | tf_op jit(solution)/shard_map/all_gather | solution.py:26
  472.2 3.0 multiply_reduce_fusion
  475.3 1.5 multiply_convert_fusion
  476.7 2.2 convolution_bitcast_fusion
  479.0 168.0 %all-reduce.3 = bf16[512,512]{0,1:T(8,128)(2,1)S(1)} all-reduce(f32[512,512]{0,1:T(8,128)} %convolution_bitcast_fusion), channel_id=1, replica_groups=mesh['aux'=4,'pair'=32] {'pair'}, use_global_device_ids=true, to_apply=%region_3.0 | all-reduce | flops 262144 | bytes 1572864 | tf_op jit(solution)/shard_map/psum | solution.py:34
  647.0 1.3 fusion.10
  648.4 3.3 bitcast_add_fusion
  651.8 66.7 %reduce-scatter.5.cloned.1.call-done = f32[2048,128]{0,1:T(8,128)} async-done(((f32[2048,512]{0,1:T(8,128)}), f32[2048,128]{0,1:T(8,128)}) %reduce-scatter.5.cloned.1.call-update) | async-done | bytes 1048592 | tf_op jit(solution)/shard_map/reduce_scatter | solution.py:49
  718.5 1.8 fusion.3
  720.3 1.0 copy.12
  (31 shorter events, 1.3 us)
Async XLA Ops:
  6.5 166.3 %copy-start = (bf16[2048,512]{1,0:T(8,128)(2,1)S(1)}, bf16[2048,512]{1,0:T(8,128)(2,1)}, u32[]{:S(2)}) copy-start(bf16[2048,512]{1,0:T(8,128)(2,1)} %param.10) | copy-start | bytes 6291460
  6.5 86.3 %copy-start.6 = (bf16[16,384]{1,0:T(8,128)(2,1)S(1)}, bf16[16,384]{1,0:T(8,128)(2,1)}, u32[]{:S(2)}) copy-start(bf16[16,384]{1,0:T(8,128)(2,1)} %param.12) | copy-start | bytes 36868
  6.5 161.8 %all-gather.3.cloned.1.call-start = ((), (), s32[]{:S(2)}) async-start(), calls=%async_computation.2 | async-start | bytes 2621440 | tf_op jit(solution)/shard_map/all_gather | solution.py:26
  7.3 431.9 %reduce-scatter.3.cloned.1.call-start = ((), (), s32[]{:S(2)}) async-start(), calls=%async_computation.3 | async-start | bytes 5242880 | tf_op jit(solution)/shard_map/reduce_scatter | solution.py:49
  168.3 4.5 copy-start.4
  337.7 2.5 copy-start.2
  343.6 4.0 copy-start.7
  343.6 128.6 %all-gather.5.cloned.1.call-start = ((), (), s32[]{:S(2)}) async-start(), calls=%async_computation.4 | async-start | bytes 2621440 | tf_op jit(solution)/shard_map/all_gather | solution.py:26
  348.4 3.9 copy-start.8
  441.9 276.6 %reduce-scatter.5.cloned.1.call-start = ((), (), s32[]{:S(2)}) async-start(), calls=%async_computation.5 | async-start | bytes 5242880 | tf_op jit(solution)/shard_map/reduce_scatter | solution.py:49
  472.2 4.5 copy-start.5
  647.0 1.4 copy-start.1
  651.8 66.7 %copy-start.3 = (bf16[2048,128]{0,1:T(8,128)(2,1)S(1)}, bf16[2048,128]{0,1:T(8,128)(2,1)}, u32[]{:S(2)}) copy-start(bf16[2048,128]{0,1:T(8,128)(2,1)} %copy.15) | copy-start | bytes 1572868
Sparse Core Ops, SparseCore 0:
  9.0 33.8 all-gather.2
  343.7 95.4 reduce-scatter.2
  442.0 30.1 all-gather.4
  651.9 66.5 reduce-scatter.4
where the time goes:
time: 728 us
  blocking collectives  492 us (68%)
  waiting for transfers between devices  184 us (25%)
  matrix products  20.9 us (3%)
  between operations  13.9 us (2%)
  local copies, waits for them, and re-layouts  9.74 us (1%)
  other arithmetic  7.65 us (1%)
    psum x2, blocking collectives, per_device(): gram = lax.psum(gram, 'pair').astype(jnp.bfloat16)  331 us
    reduce_scatter x2, waiting for transfers between devices, per_device(): share = lax.psum_scatter(part, 'aux', scatter_dimension=1, tiled=True)  153 us
    all_gather x1, blocking collectives, per_device(): lax.all_gather(thc_left, 'pair', axis=0, tiled=True)  85.5 us
    all_gather x1, blocking collectives, per_device(): lax.all_gather(thc_right, 'pair', axis=0, tiled=True)  75.5 us
    all_gather x2, waiting for transfers between devices, per_device(): whole = lax.all_gather(local, 'aux', axis=1, tiled=True)  30.3 us
  transfers between devices with their start and end apart: 4, of which 3 were waited for; matrix products, arithmetic and copies ran while one was open for 1% of the time, Pallas kernels for 0%

commit v1 on v0

--- a/solution.py
+++ b/solution.py
@@ -26,7 +26,9 @@
         whole = lax.all_gather(local, "aux", axis=1, tiled=True)
         left, right = (
             lax.all_gather(thc_left, "pair", axis=0, tiled=True),
-            lax.all_gather(thc_right, "pair", axis=0, tiled=True),
+            jnp.concatenate(
+                lax.all_to_all(jnp.stack([thc_right] * lax.axis_size("pair")), "pair", 0, 0), axis=0
+            ),
         )
         gram = lax.dot_general(
             df_factors, whole, (((0,), (0,)), ((), ())), preferred_element_type=jnp.float32

time: 728 us -> 656 us (0.901)
  blocking collectives: 492 us -> 413 us
  waiting for transfers between devices: 184 us -> 171 us
  starting transfers between devices: 0.12 us -> 11.5 us
    all_gather x1 -> x0, blocking collectives: 75.5 us -> none  [per_device(): lax.all_gather(thc_right, 'pair', axis=0, tiled=True)]
    reduce_scatter x2, waiting for transfers between devices: 153 us -> 140 us  [per_device(): share = lax.psum_scatter(part, 'aux', scatter_dimension=1, tiled=True)]
    all_to_all x0 -> x1, starting transfers between devices: none -> 11.3 us  [per_device(): lax.all_to_all(jnp.stack([thc_right] * lax.axis_size('pair')), 'pair', 0, 0)]
  transfers between devices with their start and end apart: 4 -> 5, of which waited for: 3 -> 3; matrix products, arithmetic and copies ran while one was open for 1% -> 1% of each run, Pallas kernels for 0% -> 0%
where the time goes in v1:
time: 656 us; the launch traced here: 655 us
  blocking collectives  413 us (63%)
  waiting for transfers between devices  171 us (26%)
  matrix products  21.9 us (3%)
  local copies, waits for them, and re-layouts  15.6 us (2%)
  between operations  14 us (2%)
  starting transfers between devices  11.5 us (2%)
  other arithmetic  7.51 us (1%)
    psum x2, blocking collectives, per_device(): gram = lax.psum(gram, 'pair').astype(jnp.bfloat16)  330 us
    reduce_scatter x2, waiting for transfers between devices, per_device(): share = lax.psum_scatter(part, 'aux', scatter_dimension=1, tiled=True)  140 us
    all_gather x1, blocking collectives, per_device(): lax.all_gather(thc_left, 'pair', axis=0, tiled=True)  83.4 us
    all_gather x2, waiting for transfers between devices, per_device(): whole = lax.all_gather(local, 'aux', axis=1, tiled=True)  30.3 us
  transfers between devices with their start and end apart: 5, of which 3 were waited for; matrix products, arithmetic and copies ran while one was open for 1% of the time, Pallas kernels for 0%

profile of v1, /device:TPU:1, one launch (start us, length us, event | category | flops | bytes accessed | tf_op | source)
XLA Modules:
  0.0 654.8 jit_solution(6842556269151338896)
XLA Ops:
  7.3 1.5 stack.2
  8.7 11.3 %all-to-all-start = ((bf16[32,16,384]{2,1,0:T(8,128)(2,1)}), bf16[32,16,384]{2,1,0:T(8,128)(2,1)S(1)}, u32[]{:S(2)}, u32[]{:S(2)}) async-start(bf16[32,16,384]{2,1,0:T(8,128)(2,1)} %stack.2), calls=%async_computation | async-start | bytes 786432 | tf_op jit(solution)/shard_map/all_to_all | solution.py:30
  20.1 83.4 %all_gather.11 = bf16[512,384]{1,0:T(8,128)(2,1)S(1)} all-gather(bf16[16,384]{1,0:T(8,128)(2,1)} %param.11), channel_id=1, replica_groups=mesh['aux'=4,'pair'=32] {'pair'}, dimensions={0}, use_global_device_ids=true | all-gather | bytes 405504 | tf_op jit(solution)/shard_map/all_gather | solution.py:28
  103.7 3.0 multiply_reduce_fusion.1
  106.7 1.5 multiply_convert_fusion.1
  108.8 2.3 fusion.9
  111.1 161.1 %all-reduce.2 = bf16[512,512]{1,0:T(8,128)(2,1)} all-reduce(f32[512,512]{1,0:T(8,128)} %fusion.9), channel_id=1, replica_groups=mesh['aux'=4,'pair'=32] {'pair'}, use_global_device_ids=true, to_apply=%region_0.0 | all-reduce | flops 262144 | bytes 1572864 | tf_op jit(solution)/shard_map/psum | solution.py:36
  272.2 2.5 fusion.11
  274.6 3.3 bitcast_add_fusion.1
  278.1 1.9 constant_dynamic-slice_fusion
  279.9 1.2 copy.17
  282.1 3.9 copy.19
  286.7 73.5 %reduce-scatter.3.cloned.1.call-done = f32[2048,128]{0,1:T(8,128)} async-done(((f32[2048,512]{0,1:T(8,128)}), f32[2048,128]{0,1:T(8,128)}) %reduce-scatter.3.cloned.1.call-update) | async-done | bytes 1048592 | tf_op jit(solution)/shard_map/reduce_scatter | solution.py:51
  360.2 2.6 fusion.1
  362.8 30.3 %all-gather.5.cloned.1.call-done = bf16[2048,512]{0,1:T(8,128)(2,1)} async-done(((bf16[2048,128]{0,1:T(8,128)(2,1)}), bf16[2048,512]{0,1:T(8,128)(2,1)}) %all-gather.5.cloned.1.call-update) | async-done | bytes 2097168 | tf_op jit(solution)/shard_map/all_gather | solution.py:26
  393.1 4.0 copy.16
  397.0 2.9 multiply_reduce_fusion
  399.9 1.5 multiply_convert_fusion
  402.1 2.2 convolution_bitcast_fusion
  404.3 168.6 %all-reduce.3 = bf16[512,512]{0,1:T(8,128)(2,1)} all-reduce(f32[512,512]{0,1:T(8,128)} %convolution_bitcast_fusion), channel_id=1, replica_groups=mesh['aux'=4,'pair'=32] {'pair'}, use_global_device_ids=true, to_apply=%region_3.0 | all-reduce | flops 262144 | bytes 1572864 | tf_op jit(solution)/shard_map/psum | solution.py:36
  572.9 2.5 fusion.10
  575.4 3.3 bitcast_add_fusion
  578.8 66.7 %reduce-scatter.5.cloned.1.call-done = f32[2048,128]{0,1:T(8,128)} async-done(((f32[2048,512]{0,1:T(8,128)}), f32[2048,128]{0,1:T(8,128)}) %reduce-scatter.5.cloned.1.call-update) | async-done | bytes 1048592 | tf_op jit(solution)/shard_map/reduce_scatter | solution.py:51
  645.5 1.8 fusion.3
  (34 shorter events, 4.3 us)
Async XLA Ops:
  6.5 101.6 %copy-start = (bf16[2048,512]{1,0:T(8,128)(2,1)S(1)}, bf16[2048,512]{1,0:T(8,128)(2,1)}, u32[]{:S(2)}) copy-start(bf16[2048,512]{1,0:T(8,128)(2,1)} %param.10) | copy-start | bytes 6291460
  6.5 97.1 %all-gather.3.cloned.1.call-start = ((), (), s32[]{:S(2)}) async-start(), calls=%async_computation.3 | async-start | bytes 2621440 | tf_op jit(solution)/shard_map/all_gather | solution.py:26
  8.7 94.9 %all-to-all-start = ((bf16[32,16,384]{2,1,0:T(8,128)(2,1)}), bf16[32,16,384]{2,1,0:T(8,128)(2,1)S(1)}, u32[]{:S(2)}, u32[]{:S(2)}) async-start(bf16[32,16,384]{2,1,0:T(8,128)(2,1)} %stack.2), calls=%async_computation | async-start | bytes 786432 | tf_op jit(solution)/shard_map/all_to_all | solution.py:30
  20.1 340.1 %reduce-scatter.3.cloned.1.call-start = ((), (), s32[]{:S(2)}) async-start(), calls=%async_computation.4 | async-start | bytes 5242880 | tf_op jit(solution)/shard_map/reduce_scatter | solution.py:51
  103.6 171.0 %copy-start.3 = (bf16[32,16,384]{2,1,0:T(8,128)(2,1)}, bf16[32,16,384]{2,1,0:T(8,128)(2,1)S(1)}, u32[]{:S(2)}) copy-start(bf16[32,16,384]{2,1,0:T(8,128)(2,1)S(1)} %all-to-all-done) | copy-start | bytes 1179652
  106.7 2.2 copy-start.8
  272.2 2.5 copy-start.2
  278.0 3.2 copy-start.6
  278.0 115.1 %all-gather.5.cloned.1.call-start = ((), (), s32[]{:S(2)}) async-start(), calls=%async_computation.5 | async-start | bytes 2621440 | tf_op jit(solution)/shard_map/all_gather | solution.py:26
  282.1 3.9 copy-start.7
  362.8 282.7 %reduce-scatter.5.cloned.1.call-start = ((), (), s32[]{:S(2)}) async-start(), calls=%async_computation.6 | async-start | bytes 5242880 | tf_op jit(solution)/shard_map/reduce_scatter | solution.py:51
  399.9 2.2 copy-start.5
  572.9 2.5 copy-start.1
  572.9 2.5 copy-start.4
Sparse Core Ops, SparseCore 0:
  9.0 35.9 all-gather.2
  278.1 82.0 reduce-scatter.2
  362.9 30.1 all-gather.4
  578.9 66.5 reduce-scatter.4

commit v2 on v0

--- a/solution.py
+++ b/solution.py
@@ -31,7 +31,7 @@
         gram = lax.dot_general(
             df_factors, whole, (((0,), (0,)), ((), ())), preferred_element_type=jnp.float32
         )
-        gram = lax.psum(gram, "pair").astype(jnp.bfloat16)
+        gram = jnp.sum(lax.all_gather(gram, "pair"), axis=0).astype(jnp.bfloat16)
         proj = jnp.dot(whole, right, preferred_element_type=jnp.float32).reshape(
             nocc_local, nvirt, right.shape[1]
         )

time: 728 us -> 762 us (1.047)
  blocking collectives: 492 us -> 166 us
  waiting for transfers between devices: 184 us -> 489 us
  local copies, waits for them, and re-layouts: 9.74 us -> 42.4 us
  other arithmetic: 7.65 us -> 26.2 us
    all_gather x0 -> x2, waiting for transfers between devices: none -> 345 us  [per_device(): gram = jnp.sum(lax.all_gather(gram, 'pair'), axis=0).astype(jnp.bfloat16)]
    psum x2 -> x0, blocking collectives: 331 us -> none  [per_device(): gram = lax.psum(gram, 'pair').astype(jnp.bfloat16)]
    reduce_scatter x2, waiting for transfers between devices: 153 us -> 77.7 us  [per_device(): share = lax.psum_scatter(part, 'aux', scatter_dimension=1, tiled=True)]
    all_gather x2, waiting for transfers between devices: 30.3 us -> 64.6 us  [per_device(): whole = lax.all_gather(local, 'aux', axis=1, tiled=True)]
    unnamed x22 -> x21, local copies, waits for them, and re-layouts: 6.15 us -> 38.8 us
    reduce_sum x0 -> x2, other arithmetic: none -> 18.5 us  [per_device(): gram = jnp.sum(lax.all_gather(gram, 'pair'), axis=0).astype(jnp.bfloat16)]
  transfers between devices with their start and end apart: 4 -> 6, of which waited for: 3 -> 6; matrix products, arithmetic and copies ran while one was open for 1% -> 2% of each run, Pallas kernels for 0% -> 0%
where the time goes in v2:
time: 762 us
  waiting for transfers between devices  489 us (64%)
  blocking collectives  166 us (22%)
  local copies, waits for them, and re-layouts  42.4 us (6%)
  other arithmetic  26.2 us (3%)
  matrix products  23.7 us (3%)
  between operations  14.3 us (2%)
    all_gather x2, waiting for transfers between devices, per_device(): gram = jnp.sum(lax.all_gather(gram, 'pair'), axis=0).astype(jnp.bfloat16)  345 us
    all_gather x1, blocking collectives, per_device(): lax.all_gather(thc_left, 'pair', axis=0, tiled=True)  85.5 us
    all_gather x1, blocking collectives, per_device(): lax.all_gather(thc_right, 'pair', axis=0, tiled=True)  80.8 us
    reduce_scatter x2, waiting for transfers between devices, per_device(): share = lax.psum_scatter(part, 'aux', scatter_dimension=1, tiled=True)  77.7 us
    all_gather x2, waiting for transfers between devices, per_device(): whole = lax.all_gather(local, 'aux', axis=1, tiled=True)  64.6 us
    unnamed x21, local copies, waits for them, and re-layouts  38.8 us
    reduce_sum x2, other arithmetic, per_device(): gram = jnp.sum(lax.all_gather(gram, 'pair'), axis=0).astype(jnp.bfloat16)  18.5 us
  transfers between devices with their start and end apart: 6, of which 6 were waited for; matrix products, arithmetic and copies ran while one was open for 2% of the time, Pallas kernels for 0%

profile of v2, /device:TPU:1, one launch (start us, length us, event | category | flops | bytes accessed | tf_op | source)
XLA Modules:
  0.0 761.7 jit_solution(1324210555599846738)
XLA Ops:
  7.3 34.3 %all-gather.7.cloned.1.call-done = bf16[2048,512]{1,0:T(8,128)(2,1)} async-done(((bf16[2048,128]{1,0:T(8,128)(2,1)}), bf16[2048,512]{1,0:T(8,128)(2,1)}) %all-gather.7.cloned.1.call-update) | async-done | bytes 2097168 | tf_op jit(solution)/shard_map/all_gather | solution.py:26
  41.6 3.8 fusion.9
  45.5 85.5 %all_gather.29 = bf16[512,384]{1,0:T(8,128)(2,1)S(1)} all-gather(bf16[16,384]{1,0:T(8,128)(2,1)S(1)} %copy-done.4), channel_id=1, replica_groups=mesh['aux'=4,'pair'=32] {'pair'}, dimensions={0}, use_global_device_ids=true | all-gather | bytes 405504 | tf_op jit(solution)/shard_map/all_gather | solution.py:28
  131.1 80.8 %all_gather.30 = bf16[512,384]{1,0:T(8,128)(2,1)S(1)} all-gather(bf16[16,384]{1,0:T(8,128)(2,1)S(1)} %copy-done.5), channel_id=1, replica_groups=mesh['aux'=4,'pair'=32] {'pair'}, dimensions={0}, use_global_device_ids=true | all-gather | bytes 405504 | tf_op jit(solution)/shard_map/all_gather | solution.py:29
  211.9 2.9 multiply_reduce_fusion.1
  214.7 1.5 multiply_convert_fusion.1
  216.2 94.1 %all-gather.11.cloned.1.call-done = f32[16384,512]{1,0:T(8,128)} async-done(((f32[512,512]{1,0:T(8,128)}), f32[16384,512]{1,0:T(8,128)}) %all-gather.11.cloned.1.call-update) | async-done | bytes 33554448 | tf_op jit(solution)/shard_map/all_gather | solution.py:34
  310.3 13.1 %reduce_sum.36 = bf16[512,512]{1,0:T(8,128)(2,1)} reduce(f32[32,512,512]{2,1,0:T(8,128)} %bitcast.44, f32[]{:T(128)} %constant.13.clone.1), dimensions={0}, to_apply=%region_0.0 | reduce | flops 8126464 | bytes 34078724 | tf_op jit(solution)/shard_map/reduce_sum | solution.py:34
  323.4 2.5 fusion.11
  325.9 3.3 bitcast_add_fusion.1
  330.0 1.9 constant_dynamic-slice_fusion
  331.9 2.1 copy.19
  334.8 4.0 copy.21
  338.8 33.6 %reduce-scatter.3.cloned.1.call-done = f32[2048,128]{0,1:T(8,128)} async-done(((f32[2048,512]{0,1:T(8,128)}), f32[2048,128]{0,1:T(8,128)}) %reduce-scatter.3.cloned.1.call-update) | async-done | bytes 1048592 | tf_op jit(solution)/shard_map/reduce_scatter | solution.py:49
  372.4 2.7 fusion.1
  375.2 30.3 %all-gather.9.cloned.1.call-done = bf16[2048,512]{0,1:T(8,128)(2,1)} async-done(((bf16[2048,128]{0,1:T(8,128)(2,1)}), bf16[2048,512]{0,1:T(8,128)(2,1)}) %all-gather.9.cloned.1.call-update) | async-done | bytes 2097168 | tf_op jit(solution)/shard_map/all_gather | solution.py:26
  405.5 3.8 convolution_bitcast_fusion
  409.6 2.9 multiply_reduce_fusion
  413.9 251.4 %all-gather.13.cloned.1.call-done = f32[16384,512]{0,1:T(8,128)} async-done(((f32[512,512]{0,1:T(8,128)}), f32[16384,512]{0,1:T(8,128)}) %all-gather.13.cloned.1.call-update) | async-done | bytes 33554448 | tf_op jit(solution)/shard_map/all_gather | solution.py:34
  665.3 32.5 %copy.22 = f32[64,8,32,512]{3,2,1,0:T(8,128)S(1)} copy(f32[64,8,32,512]{3,1,2,0:T(8,128)} %bitcast.45) | data formatting | bytes 67108864
  697.8 5.4 bitcast_reduce_fusion
  704.6 3.3 bitcast_add_fusion
  707.9 44.2 %reduce-scatter.5.cloned.1.call-done = f32[2048,128]{0,1:T(8,128)} async-done(((f32[2048,512]{0,1:T(8,128)}), f32[2048,128]{0,1:T(8,128)}) %reduce-scatter.5.cloned.1.call-update) | async-done | bytes 1048592 | tf_op jit(solution)/shard_map/reduce_scatter | solution.py:49
  752.1 1.8 fusion.3
  (36 shorter events, 6.1 us)
Async XLA Ops:
  6.5 35.1 %copy-start = (bf16[2048,512]{1,0:T(8,128)(2,1)S(1)}, bf16[2048,512]{1,0:T(8,128)(2,1)}, u32[]{:S(2)}) copy-start(bf16[2048,512]{1,0:T(8,128)(2,1)} %param.10) | copy-start | bytes 6291460
  6.5 35.1 %all-gather.7.cloned.1.call-start = ((), (), s32[]{:S(2)}) async-start(), calls=%async_computation.2 | async-start | bytes 2621440 | tf_op jit(solution)/shard_map/all_gather | solution.py:26
  7.3 38.3 %copy-start.4 = (bf16[16,384]{1,0:T(8,128)(2,1)S(1)}, bf16[16,384]{1,0:T(8,128)(2,1)}, u32[]{:S(2)}) copy-start(bf16[16,384]{1,0:T(8,128)(2,1)} %param.11) | copy-start | bytes 36868
  7.3 303.0 %all-gather.11.cloned.1.call-start = ((), (), s32[]{:S(2)}) async-start(), calls=%async_computation.6 | async-start | bytes 34603008 | tf_op jit(solution)/shard_map/all_gather | solution.py:34
  45.4 85.6 %copy-start.5 = (bf16[16,384]{1,0:T(8,128)(2,1)S(1)}, bf16[16,384]{1,0:T(8,128)(2,1)}, u32[]{:S(2)}) copy-start(bf16[16,384]{1,0:T(8,128)(2,1)} %param.12) | copy-start | bytes 36868
  45.5 326.9 %reduce-scatter.3.cloned.1.call-start = ((), (), s32[]{:S(2)}) async-start(), calls=%async_computation.3 | async-start | bytes 5242880 | tf_op jit(solution)/shard_map/reduce_scatter | solution.py:49
  323.4 2.5 copy-start.2
  329.2 0.7 copy-start.7
  329.2 4.7 copy-start.6
  329.2 76.2 %all-gather.9.cloned.1.call-start = ((), (), s32[]{:S(2)}) async-start(), calls=%async_computation.4 | async-start | bytes 2621440 | tf_op jit(solution)/shard_map/all_gather | solution.py:26
  375.1 290.1 %all-gather.13.cloned.1.call-start = ((), (), s32[]{:S(2)}) async-start(), calls=%async_computation.7 | async-start | bytes 34603008 | tf_op jit(solution)/shard_map/all_gather | solution.py:34
  409.3 342.8 %reduce-scatter.5.cloned.1.call-start = ((), (), s32[]{:S(2)}) async-start(), calls=%async_computation.5 | async-start | bytes 5242880 | tf_op jit(solution)/shard_map/reduce_scatter | solution.py:49
  703.2 1.4 copy-start.1
  707.9 44.2 %copy-start.3 = (bf16[2048,128]{0,1:T(8,128)(2,1)S(1)}, bf16[2048,128]{0,1:T(8,128)(2,1)}, u32[]{:S(2)}) copy-start(bf16[2048,128]{0,1:T(8,128)(2,1)} %copy.19) | copy-start | bytes 1572868
Sparse Core Ops, SparseCore 0:
  9.0 32.5 all-gather.6
  45.6 264.6 all-gather.10
  329.3 43.0 reduce-scatter.2
  375.3 30.1 all-gather.8
  409.4 255.7 all-gather.12
  708.1 43.9 reduce-scatter.4
